TPU v7x, 512 devices: a whole 4x4x16 slice. The times are simulated.
512 devices in a mesh: section: 4 (over y_hi, core), fsdp: 32 (over y_lo, z), ep: 4 (over x).
Axes of the slice: x: 4, y: 4 (y_hi: 2, y_lo: 2; y = y_hi * 2 + y_lo), z: 16, core: 2. Of those that a mesh axis runs over, the one named last changes fastest.
Arguments:
- hidden: bfloat16 [32768, 7168], P(('section', 'fsdp'), 'ep'), may hold values from -6 to 6
- attn_gain: float32 [7168], replicated, may hold values from 0.25 to 1.75
- q_gain: float32 [1536], replicated, may hold values from 0.25 to 1.75
- kv_gain: float32 [512], replicated, may hold values from 0.25 to 1.75
- down_weight: bfloat16 [7168, 2112], P('fsdp', 'ep'), may hold values from -0.0625 to 0.0625
Outputs:
- q_latent: bfloat16 [32768, 1536], P(('section', 'fsdp', 'ep'))
- kv_cache: bfloat16 [32768, 576], P(('section', 'fsdp', 'ep'))
All inputs are finite; a program needn't handle non-finite values.
Results may differ from a plain program's by a relative error of at most 0.0049.
Values may be sent and summed in bfloat16 or wider, within the bound.
A program may use at most 64 MiB of HBM per device.

v0:
```python
import jax
import jax.numpy as jnp
from jax import lax
from jax.sharding import PartitionSpec as P

QL = 1536
KVL = 512
ROPE = 64
LENGTH = 4096


epsilon = 1e-06
rope_base = 10000.0


def from_behind(x, axis, by):
    count = lax.axis_size(axis)
    return lax.ppermute(x, axis, [(i, (i + by) % count) for i in range(count)])


def root_scale(values, gain):
    mean_square = jnp.mean(values * values, axis=-1, keepdims=True)
    return values * lax.rsqrt(mean_square + epsilon) * gain


def rotate(latent, position):
    half_rope = ROPE // 2
    frequency = rope_base ** (-(jnp.arange(half_rope).astype(jnp.float32) / half_rope))
    angle = position.astype(jnp.float32)[:, None] * frequency[None, :]
    first = latent[:, QL + KVL : QL + KVL + half_rope]
    second = latent[:, QL + KVL + half_rope :]
    cosine = jnp.cos(angle)
    sine = jnp.sin(angle)
    return jnp.concatenate([first * cosine - second * sine, second * cosine + first * sine], axis=1)


def on_device(hidden, attn_gain, q_gain, kv_gain, down_weight):
    row_count = hidden.shape[0]
    moved = from_behind(hidden, "section", 1)
    whole = lax.all_gather(moved, "ep", axis=1, tiled=True)
    normed = root_scale(whole.astype(jnp.float32), attn_gain).astype(jnp.bfloat16)
    partial_latent = jnp.dot(
        normed,
        lax.all_gather(down_weight, "fsdp", axis=0, tiled=True),
        preferred_element_type=jnp.float32,
    )
    latent = lax.all_to_all(partial_latent, "ep", split_axis=0, concat_axis=1, tiled=True)
    quarter = latent.shape[0]
    query = root_scale(latent[:, :QL], q_gain).astype(jnp.bfloat16)
    key_value = root_scale(latent[:, QL : QL + KVL], kv_gain)
    row_index = (
        lax.axis_index("fsdp") * row_count + lax.axis_index("ep") * quarter + jnp.arange(quarter)
    )
    position = row_index % LENGTH
    cache = jnp.concatenate([key_value, rotate(latent, position)], axis=1).astype(jnp.bfloat16)
    return (query, cache)


def solution(mesh):
    placed = (P(("section", "fsdp"), "ep"), P(), P(), P(), P("fsdp", "ep"))
    return jax.shard_map(
        on_device,
        mesh=mesh,
        in_specs=placed,
        out_specs=(P(("section", "fsdp", "ep"), None), P(("section", "fsdp", "ep"), None)),
        check_vma=False,
    )
```

profile of v0, /device:TPU:6, one launch (start us, length us, event | category | flops | bytes accessed | tf_op | source)
XLA Modules:
  0.0 286.8 jit_solution(6684082173452654898)
XLA Ops:
  7.2 1.9 collective-permute-start
  9.1 14.5 %collective-permute-done = bf16[256,1792]{1,0:T(8,128)(2,1)S(1)} collective-permute-done((bf16[256,1792]{1,0:T(8,128)(2,1)}, bf16[256,1792]{1,0:T(8,128)(2,1)S(1)}, u32[]{:S(2)}, u32[]{:S(2)}) %collective-permute-start) | collective-permute-done | bytes 917536 | tf_op jit(solution)/shard_map/ppermute | solution.py:18
  23.6 1.0 copy-done
  24.7 0.7 all-gather.6.cloned.1.call-update
  25.4 53.5 %all-gather.4.cloned.1.call-done = bf16[256,7168]{1,0:T(8,128)(2,1)} async-done(((bf16[256,1792]{1,0:T(8,128)(2,1)}), bf16[256,7168]{1,0:T(8,128)(2,1)}) %all-gather.4.cloned.1.call-update) | async-done | bytes 3670032 | tf_op jit(solution)/shard_map/all_gather | solution.py:40
  78.9 2.8 fusion
  81.8 148.7 %all-gather.6.cloned.1.call-done = bf16[32,224,528]{1,2,0:T(8,128)(2,1)} async-done(((bf16[1,224,528]{1,2,0:T(8,128)(2,1)}), bf16[32,224,528]{1,2,0:T(8,128)(2,1)}) %all-gather.6.cloned.1.call-update) | async-done | bytes 7569424 | tf_op jit(solution)/shard_map/all_gather | solution.py:44
  230.4 9.9 %copy.16 = bf16[32,224,528]{1,0,2:T(8,128)(2,1)} copy(bf16[32,224,528]{1,2,0:T(8,128)(2,1)} %all-gather.6.cloned.1.call-done) | data formatting | bytes 15138816 | tf_op jit(solution)/shard_map/all_gather | solution.py:44
  240.3 16.7 %reshape.58 = bf16[7168,528]{0,1:T(8,128)(2,1)} reshape(bf16[32,224,528]{1,0,2:T(8,128)(2,1)} %copy.16) | data formatting | bytes 15138816
  257.0 8.2 %fusion.3 = f32[256,528]{1,0:T(8,128)} fusion(bf16[7168,528]{0,1:T(8,128)(2,1)} %reshape.58, bf16[256,7168]{1,0:T(8,128)(2,1)} %all-gather.4.cloned.1.call-done, f32[7168]{0:T(1024)S(1)} %copy-done.3, f32[256]{0:T(256)S(1)} %add_rsqrt_fusion), kind=kOutput, calls=%fused_computation.5 | convolution fusion | flops 1945108480 | bytes 11809792 | tf_op jit(solution)/shard_map/dot_general | solution.py:42
  265.2 4.8 %all-to-all-start = ((f32[4,64,528]{2,1,0:T(8,128)}), f32[4,64,528]{2,1,0:T(8,128)S(1)}, u32[]{:S(2)}, u32[]{:S(2)}) async-start(f32[4,64,528]{2,1,0:T(8,128)} %bitcast.1), calls=%async_computation | async-start | bytes 1310720 | tf_op jit(solution)/shard_map/all_to_all | solution.py:47
  270.0 6.7 %all-to-all-done = f32[4,64,528]{2,1,0:T(8,128)S(1)} async-done(((f32[4,64,528]{2,1,0:T(8,128)}), f32[4,64,528]{2,1,0:T(8,128)S(1)}, u32[]{:S(2)}, u32[]{:S(2)}) %all-to-all-start) | async-done | bytes 540704 | tf_op jit(solution)/shard_map/all_to_all | solution.py:47
  276.7 0.4 copy.18
  277.2 0.3 all_to_all.17
  277.5 0.1 multiply_reduce_fusion
  277.6 0.1 fusion.17
  277.7 0.1 multiply_reduce_fusion.1
  277.9 0.1 copy.24
  278.0 0.2 fusion.12
  278.1 0.1 copy.22
  278.2 0.1 copy.21
  278.4 0.8 multiply_convert_fusion
  279.1 0.1 multiply_convert_fusion.1
  279.2 0.7 pad_maximum_fusion
  (16 shorter events, 0.2 us)
Async XLA Ops:
  7.2 71.7 %all-gather.4.cloned.1.call-start = ((), (), s32[]{:S(2)}) async-start(), calls=%async_computation.1 | async-start | bytes 4587520 | tf_op jit(solution)/shard_map/all_gather | solution.py:40
  7.2 16.4 %collective-permute-start = (bf16[256,1792]{1,0:T(8,128)(2,1)}, bf16[256,1792]{1,0:T(8,128)(2,1)S(1)}, u32[]{:S(2)}, u32[]{:S(2)}) collective-permute-start(bf16[256,1792]{1,0:T(8,128)(2,1)} %param.5), channel_id=1, source_target_pairs={{0,128},{128,256},{256,384},{384,0},{1,129},{129,257},{257,385},{3... | collective-permute-start | bytes 2752520 | tf_op jit(solution)/shard_map/ppermute | solution.py:18
  23.6 1.0 copy-start
  24.7 205.8 %all-gather.6.cloned.1.call-start = ((), (), s32[]{:S(2)}) async-start(), calls=%async_computation.2 | async-start | bytes 8921088 | tf_op jit(solution)/shard_map/all_gather | solution.py:44
  240.3 16.7 %copy-start.3 = (f32[7168]{0:T(1024)S(1)}, f32[7168]{0:T(1024)}, u32[]{:S(2)}) copy-start(f32[7168]{0:T(1024)} %param.6) | copy-start | bytes 86020
  257.0 21.4 %copy-start.1 = (f32[1536]{0:T(1024)S(1)}, f32[1536]{0:T(1024)}, u32[]{:S(2)}) copy-start(f32[1536]{0:T(1024)} %param.7) | copy-start | bytes 18436
  257.0 22.2 %copy-start.2 = (f32[512]{0:T(512)S(1)}, f32[512]{0:T(512)}, u32[]{:S(2)}) copy-start(f32[512]{0:T(512)} %param.8) | copy-start | bytes 6148
  265.2 11.5 %all-to-all-start = ((f32[4,64,528]{2,1,0:T(8,128)}), f32[4,64,528]{2,1,0:T(8,128)S(1)}, u32[]{:S(2)}, u32[]{:S(2)}) async-start(f32[4,64,528]{2,1,0:T(8,128)} %bitcast.1), calls=%async_computation | async-start | bytes 1310720 | tf_op jit(solution)/shard_map/all_to_all | solution.py:47
Sparse Core Ops, SparseCore 0:
  24.8 54.0 all-gather.3
  81.0 149.4 all-gather.5
where the time goes:
time: 289 us; the launch traced here: 287 us
  waiting for transfers between devices  224 us (78%)
  local copies, waits for them, and re-layouts  28.7 us (10%)
  between operations  14.1 us (5%)
  matrix products  8.22 us (3%)
  starting transfers between devices  6.8 us (2%)
  other arithmetic  4.86 us (2%)
    all_gather x1, waiting for transfers between devices, on_device(): lax.all_gather(down_weight, 'fsdp', axis=0, tiled=True)  149 us
    all_gather x1, waiting for transfers between devices, on_device(): whole = lax.all_gather(moved, 'ep', axis=1, tiled=True)  53.5 us
    unnamed x11, local copies, waits for them, and re-layouts  17.8 us
    ppermute x1, waiting for transfers between devices, from_behind(): return lax.ppermute(x, axis, [(i, (i + by) % count) for i in range(count)])  14.5 us
    all_gather x1, local copies, waits for them, and re-layouts, on_device(): lax.all_gather(down_weight, 'fsdp', axis=0, tiled=True)  9.89 us
    dot_general x1, matrix products, on_device(): jnp.dot(normed, lax.all_gather(down_weight, 'fsdp', axis=0, tiled=True),...  8.22 us
    all_to_all x1, waiting for transfers between devices, on_device(): lax.all_to_all(partial_latent, 'ep', split_axis=0, concat_axis=1, tiled=T...  6.7 us
  transfers between devices with their start and end apart: 4, of which 4 were waited for; matrix products, arithmetic and copies ran while one was open for 1% of the time, Pallas kernels for 0%

commit v1 on v0

v1 whole, which is shorter than its diff:
```python
import functools

import jax
import jax.numpy as jnp
from jax import lax
from jax.experimental import pallas as pl
from jax.experimental.pallas import tpu as pltpu
from jax.sharding import PartitionSpec as P

MESH = pl.DeviceIdType.MESH

QL = 1536
KVL = 512
ROPE = 64
LENGTH = 4096
D = 7168

epsilon = 1e-06
rope_base = 10000.0

ROWS = 256
KS = 1792
WR = 224
WC = 528
PARTS = 2
PR = WR // PARTS
HALF = ROWS // 2
QUARTER = ROWS // 4
WIDE = 640
NZ = 16
HOPS = NZ // 2


def kernel(
    hid, w, gain, q_gain, kv_gain, cosine, sine, q_out, kv_out,
    xbuf, xg, wbuf, acc, ssq, lsend, lrecv,
    local_sem, xs, xr, zs, zr, ys, yr, cs, cr, ls, lr,
):
    sec = lax.axis_index("section")
    f = lax.axis_index("fsdp")
    x = lax.axis_index("ep")
    core = sec % 2
    yl = f // NZ
    z = f % NZ
    y = (sec // 2) * 2 + yl
    way = 1 - 2 * core

    def place(y_, z_, core_, x_):
        y_ = (y_ + 8) % 4
        z_ = (z_ + 2 * NZ) % NZ
        return ((y_ // 2) * 2 + core_, (y_ % 2) * NZ + z_, (x_ + 4) % 4)

    ahead_z = place(y, z + way, core, x)
    ahead_y = place(y + way, z, core, x)
    sibling = place(y, z, 1 - core, x)
    right = place(y, z, core, x + 1)
    left = place(y, z, core, x - 1)

    barrier = pltpu.get_barrier_semaphore()
    partners = [
        place(y, z + 1, core, x), place(y, z - 1, core, x),
        place(y + 1, z, core, x), place(y - 1, z, core, x),
        sibling, right, left,
    ]
    for other in range(4):
        partners.append(((sec + 1) % 4, f, other))
        partners.append(((sec + 3) % 4, f, other))
    for partner in partners:
        pl.semaphore_signal(barrier, inc=1, device_id=partner, device_id_type=MESH)
    pl.semaphore_wait(barrier, len(partners))

    def rdma(src, dst, send, recv, device):
        return pltpu.make_async_remote_copy(
            src_ref=src, dst_ref=dst, send_sem=send, recv_sem=recv,
            device_id=device, device_id_type=MESH,
        )

    sends = []

    def start(copy):
        copy.start()
        sends.append(copy)

    def x_rows(owner, half):
        return xbuf.at[owner, pl.ds(half * HALF, HALF)]

    def x_own(half, index, device):
        return rdma(hid.at[pl.ds(half * HALF, HALF)], x_rows(x, half), xs.at[index], xr.at[index], device)

    x_left, x_right, x_far = (x + 3) % 4, (x + 1) % 4, (x + 2) % 4

    def w_rows(slot, part):
        return wbuf.at[pl.ds(pl.multiple_of(slot * WR + part * PR, PR), PR)]

    def ring_slot(d):
        return yl * NZ + (z - way * d + NZ) % NZ

    def pair_slot(j):
        return (1 - yl) * NZ + (z - way * (j + 1 - core) + NZ) % NZ

    def cross_ring_slot(d):
        return yl * NZ + (z + way * d + NZ) % NZ

    def cross_pair_slot(j):
        return (1 - yl) * NZ + (z + way * (j + core) + NZ) % NZ

    def w_src(d, part):
        if d == 0:
            return w.at[pl.ds(part * PR, PR)]
        return w_rows(ring_slot(d), part)

    own_x = pltpu.make_async_copy(hid, xbuf.at[x], local_sem.at[0])
    own_w = pltpu.make_async_copy(w, wbuf.at[pl.ds(pl.multiple_of(f * WR, WR), WR)], local_sem.at[1])

    def z_copy(d, part):
        i = d * PARTS + part
        return rdma(w_src(d, part), w_rows(ring_slot(d), part), zs.at[i], zr.at[i], ahead_z)

    def y_copy(d, part):
        i = (d - 1 + core) * PARTS + part
        return rdma(w_src(d, part), w_rows(ring_slot(d), part), ys.at[i], yr.at[i], ahead_y)

    def cross_ring(d, part):
        i = (d - 1) * PARTS + part
        rows = w_rows(ring_slot(d), part)
        return rdma(rows, rows, cs.at[i], cr.at[i], sibling)

    def cross_pair(j, part):
        i = (HOPS - 1 + j) * PARTS + part
        rows = w_rows(pair_slot(j), part)
        return rdma(rows, rows, cs.at[i], cr.at[i], sibling)

    def hand_on_pair(j):
        for part in range(PARTS):
            i = j * PARTS + part
            rows = w_rows(pair_slot(j), part)
            rdma(rows, rows, ys.at[i], yr.at[i], ahead_y).wait_recv()
            start(cross_pair(j, part))

    def prepare(owner, half):
        g = gain[owner]

        def block(i, carry):
            rows = pl.ds(pl.multiple_of(half * HALF + i * 16, 16), 16)
            v = xbuf[owner, rows, :].astype(jnp.float32)
            xg[owner, rows, :] = (v * g).astype(jnp.bfloat16)
            total = ssq[rows, :]
            for t in range(KS // 128):
                piece = v[:, t * 128 : (t + 1) * 128]
                total = total + piece * piece
            ssq[rows, :] = total
            return carry

        lax.fori_loop(0, HALF // 16, block, 0)

    def multiply(owner):
        columns = wbuf[pl.ds(pl.multiple_of(owner * KS, KS), KS), :]
        for half in range(2):
            rows = pl.ds(half * HALF, HALF)
            acc[rows, :WC] += jnp.dot(xg[owner, rows, :], columns, preferred_element_type=jnp.float32)

    for part in range(PARTS):
        start(z_copy(0, part))

        @pl.when(core == 1)
        def _():
            y_copy(0, part).start()

    start(x_own(0, 0, right))
    start(x_own(1, 1, left))
    start(x_own(1, 2, right))
    start(x_own(0, 3, left))
    own_x.start()
    own_w.start()
    ssq[...] = jnp.zeros_like(ssq)
    acc[...] = jnp.zeros_like(acc)
    own_x.wait()
    prepare(x, 0)
    prepare(x, 1)
    own_w.wait()

    for d in range(1, HOPS + 1):
        for part in range(PARTS):
            z_copy(d - 1, part).wait_recv()
            if d < HOPS:
                start(z_copy(d, part))
                y_copy(d, part).start()
                start(cross_ring(d, part))
            else:

                @pl.when(core == 0)
                def _():
                    y_copy(d, part).start()

        if d >= 3:
            hand_on_pair(d - 3)
        if d == HOPS - 2:
            x_own(0, 0, right).wait_recv()
            start(rdma(x_rows(x_left, 0), x_rows(x_left, 0), xs.at[4], xr.at[4], right))
            x_own(1, 1, left).wait_recv()
            start(rdma(x_rows(x_right, 1), x_rows(x_right, 1), xs.at[5], xr.at[5], left))
            prepare(x_left, 0)
            prepare(x_right, 1)
    hand_on_pair(HOPS - 2)
    hand_on_pair(HOPS - 1)

    x_own(1, 2, right).wait_recv()
    prepare(x_left, 1)
    x_own(0, 3, left).wait_recv()
    prepare(x_right, 0)

    for i in range((2 * HOPS - 1) * PARTS):
        rows = w_rows(0, 0)
        rdma(rows, rows, cs.at[i], cr.at[i], sibling).wait_recv()

    def slice_step(i, carry):
        multiply(lax.rem(x_left + i, 4))
        return carry

    lax.fori_loop(0, 3, slice_step, 0)

    for half in range(2):
        rows = x_rows(x_far, half)
        rdma(rows, rows, xs.at[4 + half], xr.at[4 + half], right).wait_recv()
        prepare(x_far, half)
    multiply(x_far)

    scale = lax.rsqrt(jnp.sum(ssq[...], axis=1, keepdims=True) / D + epsilon)
    out = pltpu.roll(acc[...] * scale, x * 16, 1).astype(jnp.bfloat16)
    for other in range(4):
        lsend[other] = out[other * QUARTER : (other + 1) * QUARTER]
    for other in range(4):
        start(rdma(lsend.at[other], lrecv.at[x], ls.at[other], lr.at[x], ((sec + 1) % 4, f, other)))
    for other in range(4):
        rdma(lsend.at[other], lrecv.at[other], ls.at[other], lr.at[other], ((sec + 1) % 4, f, other)).wait_recv()

    pieces = [lrecv[other].astype(jnp.float32) for other in range(4)]
    tiles = []
    for other in range(4):
        first = pieces[other][:, :128]
        if other:
            first = first + pieces[other - 1][:, 512:]
        tiles.append(first)
        tiles.append(pieces[other][:, 128:512])
    latent = jnp.concatenate(tiles, axis=1)
    rope = pieces[3][:, 512:]

    q = latent[:, :QL]
    q_out[...] = (
        q * lax.rsqrt(jnp.mean(q * q, axis=1, keepdims=True) + epsilon) * q_gain[...]
    ).astype(jnp.bfloat16)
    k = latent[:, QL:]
    kv_out[:, :KVL] = (
        k * lax.rsqrt(jnp.mean(k * k, axis=1, keepdims=True) + epsilon) * kv_gain[...]
    ).astype(jnp.bfloat16)
    lane = lax.broadcasted_iota(jnp.int32, rope.shape, 1)
    swapped = jnp.where(lane < ROPE // 2, pltpu.roll(rope, 128 - ROPE // 2, 1), pltpu.roll(rope, ROPE // 2, 1))
    turned = rope * cosine[...] + swapped * sine[...]
    kv_out[:, KVL:] = turned[:, :ROPE].astype(jnp.bfloat16)

    for copy in sends:
        copy.wait_send()
    for i in range(HOPS * PARTS):
        rows = w_rows(0, 0)
        rdma(rows, rows, ys.at[i], yr.at[i], ahead_y).wait_send()


def on_device(hidden, attn_gain, q_gain, kv_gain, down_weight):
    quarter = QUARTER
    half_rope = ROPE // 2
    row_index = lax.axis_index("fsdp") * ROWS + lax.axis_index("ep") * quarter + jnp.arange(quarter)
    position = row_index % LENGTH
    frequency = rope_base ** (-(jnp.arange(half_rope).astype(jnp.float32) / half_rope))
    angle = position.astype(jnp.float32)[:, None] * frequency[None, :]
    cosine, sine = jnp.cos(angle), jnp.sin(angle)
    rest = jnp.zeros((quarter, 128 - ROPE), jnp.float32)
    cosine = jnp.concatenate([cosine, cosine, rest], axis=1)
    sine = jnp.concatenate([-sine, sine, rest], axis=1)

    vmem = pl.BlockSpec(memory_space=pltpu.VMEM)
    hbm = pl.BlockSpec(memory_space=pl.ANY)
    dma = pltpu.SemaphoreType.DMA
    return pl.pallas_call(
        kernel,
        out_shape=(
            jax.ShapeDtypeStruct((quarter, QL), jnp.bfloat16),
            jax.ShapeDtypeStruct((quarter, KVL + ROPE), jnp.bfloat16),
        ),
        in_specs=[hbm, hbm, vmem, vmem, vmem, vmem, vmem],
        out_specs=(vmem, vmem),
        scratch_shapes=[
            pltpu.VMEM((4, ROWS, KS), jnp.bfloat16),
            pltpu.VMEM((4, ROWS, KS), jnp.bfloat16),
            pltpu.VMEM((D, WC), jnp.bfloat16),
            pltpu.VMEM((ROWS, WIDE), jnp.float32),
            pltpu.VMEM((ROWS, 128), jnp.float32),
            pltpu.VMEM((4, QUARTER, WIDE), jnp.bfloat16),
            pltpu.VMEM((4, QUARTER, WIDE), jnp.bfloat16),
            dma((2,)),
            dma((6,)), dma((6,)),
            dma((HOPS * PARTS,)), dma((HOPS * PARTS,)),
            dma((HOPS * PARTS,)), dma((HOPS * PARTS,)),
            dma(((2 * HOPS - 1) * PARTS,)), dma(((2 * HOPS - 1) * PARTS,)),
            dma((4,)), dma((4,)),
        ],
        compiler_params=pltpu.CompilerParams(collective_id=0, has_side_effects=True, vmem_limit_bytes=50 * 2**20),
    )(
        hidden, down_weight, attn_gain.reshape(4, 1, KS), q_gain.reshape(1, QL), kv_gain.reshape(1, KVL), cosine, sine,
    )


def solution(mesh):
    placed = (P(("section", "fsdp"), "ep"), P(), P(), P(), P("fsdp", "ep"))
    return jax.shard_map(
        on_device,
        mesh=mesh,
        in_specs=placed,
        out_specs=(P(("section", "fsdp", "ep"), None), P(("section", "fsdp", "ep"), None)),
        check_vma=False,
    )
```

time: 289 us -> 72.7 us (0.25)
  waiting for transfers between devices: 224 us -> 0 us
  Pallas kernels: 0 us -> 67 us
  local copies, waits for them, and re-layouts: 28.7 us -> 4.02 us
  between operations: 14.1 us -> 0.71 us
  matrix products: 8.22 us -> 0 us
  starting transfers between devices: 6.8 us -> 0 us
  other arithmetic: 4.86 us -> 0.3 us
    all_gather x2 -> x0, waiting for transfers between devices: 202 us -> none  [the longest x1 149 us: on_device(): lax.all_gather(down_weight, 'fsdp', axis=0, tiled=True)]
    pallas_call x0 -> x1, Pallas kernels: none -> 67 us  [on_device(): pl.pallas_call(kernel, out_shape=(jax.ShapeDtypeStruct((quarter, QL), jnp...]
    unnamed x11, local copies, waits for them, and re-layouts: 17.8 us -> 3.23 us
    ppermute x1 -> x0, waiting for transfers between devices: 14.5 us -> none  [from_behind(): return lax.ppermute(x, axis, [(i, (i + by) % count) for i in range(count)])]
    all_gather x1 -> x0, local copies, waits for them, and re-layouts: 9.89 us -> none  [on_device(): lax.all_gather(down_weight, 'fsdp', axis=0, tiled=True)]
    dot_general x1 -> x0, matrix products: 8.22 us -> none  [on_device(): jnp.dot(normed, lax.all_gather(down_weight, 'fsdp', axis=0, tiled=True),...]
    all_to_all x1 -> x0, waiting for transfers between devices: 6.7 us -> none  [on_device(): lax.all_to_all(partial_latent, 'ep', split_axis=0, concat_axis=1, tiled=T...]
    all_to_all x1 -> x0, starting transfers between devices: 4.8 us -> none  [on_device(): lax.all_to_all(partial_latent, 'ep', split_axis=0, concat_axis=1, tiled=T...]
  transfers between devices with their start and end apart: 4 -> 0, of which waited for: 4 -> 0; matrix products, arithmetic and copies ran while one was open for 1% -> 0% of each run, Pallas kernels for 0% -> 0%
where the time goes in v1:
time: 72.7 us; the launch traced here: 72 us
  Pallas kernels  67 us (92%)
  local copies, waits for them, and re-layouts  4.02 us (6%)
    pallas_call x1, Pallas kernels, on_device(): pl.pallas_call(kernel, out_shape=(jax.ShapeDtypeStruct((quarter, QL), jnp...  67 us
    unnamed x11, local copies, waits for them, and re-layouts  3.23 us

profile of v1, /device:TPU:6, one launch (start us, length us, event | category | flops | bytes accessed | tf_op | source)
XLA Modules:
  0.0 72.0 jit_solution(17547989664410686300)
XLA Ops:
  0.6 0.0 copy-start.3
  0.7 0.1 pad.5.clone
  0.8 0.7 reshape.37.q_gain
  1.5 0.2 fusion
  1.7 0.1 maximum_maximum_fusion.1
  1.8 0.0 copy-done.3
  1.8 0.0 copy-start.1
  1.8 0.0 copy-start.2
  1.8 0.2 copy.7.w
  2.0 0.5 copy-done.1
  2.5 0.0 copy-done.2
  2.5 0.0 copy-start
  2.5 1.2 %copy-done = bf16[256,1792]{1,0:T(8,128)(2,1)S(1)} copy-done((bf16[256,1792]{1,0:T(8,128)(2,1)S(1)}, bf16[256,1792]{1,0:T(8,128)(2,1)}, u32[]{:S(2)}) %copy-start) | copy-done | bytes 917528
  3.7 67.0 %shard_map.68 = (bf16[64,1536]{1,0:T(8,128)(2,1)S(1)}, bf16[64,576]{1,0:T(8,128)(2,1)S(1)}) custom-call(bf16[256,1792]{1,0:T(8,128)(2,1)S(1)} %copy-done, bf16[224,528]{1,0:T(8,128)(2,1)S(1)} %copy.7.w, f32[4,1,1792]{2,1,0:T(1,128)S(1)} %bitcast.2, f32[1,1536]{1,0:T(1,128)S(1)} %reshape.37.q_gain, f32[1,512]{1,0:T(1,128)S(1)} %bitcast.3, ...), custom_call_target="tpu_custom_call" | custom-call | tf_op jit(solution)/shard_map/pallas_call | solution.py:283
  70.7 0.7 copy.10
  71.3 0.6 copy.11
  (3 shorter events, 0.0 us)
Async XLA Ops:
  0.6 1.1 %copy-start.3 = (bf16[224,528]{0,1:T(8,128)(2,1)S(1)}, bf16[224,528]{0,1:T(8,128)(2,1)}, u32[]{:S(2)}) copy-start(bf16[224,528]{0,1:T(8,128)(2,1)} %param.9) | copy-start | bytes 709636
  1.8 0.8 %copy-start.1 = (f32[7168]{0:T(1024)S(1)}, f32[7168]{0:T(1024)}, u32[]{:S(2)}) copy-start(f32[7168]{0:T(1024)} %param.6) | copy-start | bytes 86020
  1.8 0.7 %copy-start.2 = (f32[512]{0:T(512)S(1)}, f32[512]{0:T(512)}, u32[]{:S(2)}) copy-start(f32[512]{0:T(512)} %param.8) | copy-start | bytes 6148
  2.5 1.2 %copy-start = (bf16[256,1792]{1,0:T(8,128)(2,1)S(1)}, bf16[256,1792]{1,0:T(8,128)(2,1)}, u32[]{:S(2)}) copy-start(bf16[256,1792]{1,0:T(8,128)(2,1)} %hid.1) | copy-start | bytes 2752516

commit v2 on v1

--- a/solution.py
+++ b/solution.py
@@ -22,7 +22,7 @@
 KS = 1792
 WR = 224
 WC = 528
-PARTS = 2
+PARTS = 7
 PR = WR // PARTS
 HALF = ROWS // 2
 QUARTER = ROWS // 4
@@ -32,9 +32,9 @@
 
 
 def kernel(
-    hid, w, gain, q_gain, kv_gain, cosine, sine, q_out, kv_out,
-    xbuf, xg, wbuf, acc, ssq, lsend, lrecv,
-    local_sem, xs, xr, zs, zr, ys, yr, cs, cr, ls, lr,
+    hid, w, gain, q_gain, kv_gain, q_out, kv_out,
+    xbuf, xg, wbuf, acc, ssq, lsend, lrecv, gain_v, q_gain_v, kv_gain_v, cosine, sine,
+    local_sem, xs, xr, zs, zr, ys, yr, cs, cr, ls, lr, rounds,
 ):
     sec = lax.axis_index("section")
     f = lax.axis_index("fsdp")
@@ -57,17 +57,24 @@
     left = place(y, z, core, x - 1)
 
     barrier = pltpu.get_barrier_semaphore()
-    partners = [
-        place(y, z + 1, core, x), place(y, z - 1, core, x),
-        place(y + 1, z, core, x), place(y - 1, z, core, x),
-        sibling, right, left,
-    ]
-    for other in range(4):
-        partners.append(((sec + 1) % 4, f, other))
-        partners.append(((sec + 3) % 4, f, other))
-    for partner in partners:
-        pl.semaphore_signal(barrier, inc=1, device_id=partner, device_id_type=MESH)
+    up_y, down_y = place(y + 1, z, core, x), place(y - 1, z, core, x)
+    partners = [place(y, z + 1, core, x), place(y, z - 1, core, x), up_y, down_y, sibling, right, left]
+
+    def tell(semaphore, devices):
+        for device in devices:
+            pl.semaphore_signal(semaphore, inc=1, device_id=device, device_id_type=MESH)
+
+    tell(barrier, partners)
     pl.semaphore_wait(barrier, len(partners))
+
+    tell(rounds.at[0], (right, left))
+
+    def next_round(n):
+        if n < 3:
+            pl.semaphore_wait(rounds.at[n], 2)
+            tell(rounds.at[n + 1], (up_y, down_y) if n < 2 else (sibling,))
+        else:
+            pl.semaphore_wait(rounds.at[n], 1)
 
     def rdma(src, dst, send, recv, device):
         return pltpu.make_async_remote_copy(
@@ -110,6 +117,11 @@
         return w_rows(ring_slot(d), part)
 
     own_x = pltpu.make_async_copy(hid, xbuf.at[x], local_sem.at[0])
+    own_gains = [
+        pltpu.make_async_copy(gain, gain_v, local_sem.at[2]),
+        pltpu.make_async_copy(q_gain, q_gain_v, local_sem.at[3]),
+        pltpu.make_async_copy(kv_gain, kv_gain_v, local_sem.at[4]),
+    ]
     own_w = pltpu.make_async_copy(w, wbuf.at[pl.ds(pl.multiple_of(f * WR, WR), WR)], local_sem.at[1])
 
     def z_copy(d, part):
@@ -120,25 +132,45 @@
         i = (d - 1 + core) * PARTS + part
         return rdma(w_src(d, part), w_rows(ring_slot(d), part), ys.at[i], yr.at[i], ahead_y)
 
-    def cross_ring(d, part):
-        i = (d - 1) * PARTS + part
-        rows = w_rows(ring_slot(d), part)
-        return rdma(rows, rows, cs.at[i], cr.at[i], sibling)
-
-    def cross_pair(j, part):
-        i = (HOPS - 1 + j) * PARTS + part
-        rows = w_rows(pair_slot(j), part)
-        return rdma(rows, rows, cs.at[i], cr.at[i], sibling)
+    def diagonal(part):
+        i = (HOPS - 1) * PARTS + part
+        rows = w_rows(ring_slot(HOPS - 1), part)
+        return rdma(rows, rows, ys.at[i], yr.at[i], place(y + way, z + way, core, x))
+
+    def shard(slot):
+        return wbuf.at[pl.ds(pl.multiple_of(slot * WR, WR), WR)]
+
+    def cross(slot, i):
+        return rdma(shard(slot), shard(slot), cs.at[i], cr.at[i], sibling)
+
+    def each_part(step):
+        def body(part, carry):
+            step(part)
+            return carry
+
+        lax.fori_loop(0, PARTS, body, 0)
 
     def hand_on_pair(j):
-        for part in range(PARTS):
+        def step(part):
             i = j * PARTS + part
             rows = w_rows(pair_slot(j), part)
             rdma(rows, rows, ys.at[i], yr.at[i], ahead_y).wait_recv()
-            start(cross_pair(j, part))
+
+        each_part(step)
+        start(cross(pair_slot(j), HOPS - 1 + j))
+
+    def angles():
+        half_rope = ROPE // 2
+        shape = (QUARTER, 128)
+        lane = lax.broadcasted_iota(jnp.int32, shape, 1)
+        row = lax.broadcasted_iota(jnp.int32, shape, 0) + f * ROWS + x * QUARTER
+        power = (lane % half_rope).astype(jnp.float32) / half_rope
+        angle = (row % LENGTH).astype(jnp.float32) * (rope_base ** (-power))
+        cosine[...] = jnp.cos(angle)
+        sine[...] = jnp.where(lane < half_rope, -jnp.sin(angle), jnp.sin(angle))
 
     def prepare(owner, half):
-        g = gain[owner]
+        g = gain_v[pl.ds(pl.multiple_of(owner * KS, KS), KS)][None, :]
 
         def block(i, carry):
             rows = pl.ds(pl.multiple_of(half * HALF + i * 16, 16), 16)
@@ -159,47 +191,61 @@
             rows = pl.ds(half * HALF, HALF)
             acc[rows, :WC] += jnp.dot(xg[owner, rows, :], columns, preferred_element_type=jnp.float32)
 
-    for part in range(PARTS):
-        start(z_copy(0, part))
+    def first(part):
+        z_copy(0, part).start()
 
         @pl.when(core == 1)
         def _():
             y_copy(0, part).start()
 
+    each_part(first)
     start(x_own(0, 0, right))
     start(x_own(1, 1, left))
     start(x_own(1, 2, right))
     start(x_own(0, 3, left))
     own_x.start()
     own_w.start()
+    for copy in own_gains:
+        copy.start()
+    angles()
     ssq[...] = jnp.zeros_like(ssq)
     acc[...] = jnp.zeros_like(acc)
     own_x.wait()
+    for copy in own_gains:
+        copy.wait()
     prepare(x, 0)
     prepare(x, 1)
     own_w.wait()
 
     for d in range(1, HOPS + 1):
-        for part in range(PARTS):
+
+        def step(part):
             z_copy(d - 1, part).wait_recv()
             if d < HOPS:
-                start(z_copy(d, part))
+                z_copy(d, part).start()
+                if d == HOPS - 1:
+
+                    @pl.when(core == 0)
+                    def _():
+                        diagonal(part).start()
+
                 y_copy(d, part).start()
-                start(cross_ring(d, part))
-            else:
-
-                @pl.when(core == 0)
-                def _():
-                    y_copy(d, part).start()
-
+
+        each_part(step)
+        if d < HOPS:
+            start(cross(ring_slot(d), d - 1))
         if d >= 3:
             hand_on_pair(d - 3)
-        if d == HOPS - 2:
+        if d <= 4:
+            next_round(d - 1)
+        if d == 5:
             x_own(0, 0, right).wait_recv()
             start(rdma(x_rows(x_left, 0), x_rows(x_left, 0), xs.at[4], xr.at[4], right))
             x_own(1, 1, left).wait_recv()
             start(rdma(x_rows(x_right, 1), x_rows(x_right, 1), xs.at[5], xr.at[5], left))
+        if d == 6:
             prepare(x_left, 0)
+        if d == 7:
             prepare(x_right, 1)
     hand_on_pair(HOPS - 2)
     hand_on_pair(HOPS - 1)
@@ -209,9 +255,8 @@
     x_own(0, 3, left).wait_recv()
     prepare(x_right, 0)
 
-    for i in range((2 * HOPS - 1) * PARTS):
-        rows = w_rows(0, 0)
-        rdma(rows, rows, cs.at[i], cr.at[i], sibling).wait_recv()
+    for i in range(2 * HOPS - 1):
+        cross(0, i).wait_recv()
 
     def slice_step(i, carry):
         multiply(lax.rem(x_left + i, 4))
@@ -247,11 +292,11 @@
 
     q = latent[:, :QL]
     q_out[...] = (
-        q * lax.rsqrt(jnp.mean(q * q, axis=1, keepdims=True) + epsilon) * q_gain[...]
+        q * lax.rsqrt(jnp.mean(q * q, axis=1, keepdims=True) + epsilon) * q_gain_v[...][None, :]
     ).astype(jnp.bfloat16)
     k = latent[:, QL:]
     kv_out[:, :KVL] = (
-        k * lax.rsqrt(jnp.mean(k * k, axis=1, keepdims=True) + epsilon) * kv_gain[...]
+        k * lax.rsqrt(jnp.mean(k * k, axis=1, keepdims=True) + epsilon) * kv_gain_v[...][None, :]
     ).astype(jnp.bfloat16)
     lane = lax.broadcasted_iota(jnp.int32, rope.shape, 1)
     swapped = jnp.where(lane < ROPE // 2, pltpu.roll(rope, 128 - ROPE // 2, 1), pltpu.roll(rope, ROPE // 2, 1))
@@ -260,25 +305,20 @@
 
     for copy in sends:
         copy.wait_send()
-    for i in range(HOPS * PARTS):
+    def sent(i, carry):
         rows = w_rows(0, 0)
+        rdma(rows, rows, zs.at[i], zr.at[i], ahead_z).wait_send()
         rdma(rows, rows, ys.at[i], yr.at[i], ahead_y).wait_send()
+        return carry
+
+    lax.fori_loop(0, HOPS * PARTS, sent, 0)
 
 
 def on_device(hidden, attn_gain, q_gain, kv_gain, down_weight):
     quarter = QUARTER
-    half_rope = ROPE // 2
-    row_index = lax.axis_index("fsdp") * ROWS + lax.axis_index("ep") * quarter + jnp.arange(quarter)
-    position = row_index % LENGTH
-    frequency = rope_base ** (-(jnp.arange(half_rope).astype(jnp.float32) / half_rope))
-    angle = position.astype(jnp.float32)[:, None] * frequency[None, :]
-    cosine, sine = jnp.cos(angle), jnp.sin(angle)
-    rest = jnp.zeros((quarter, 128 - ROPE), jnp.float32)
-    cosine = jnp.concatenate([cosine, cosine, rest], axis=1)
-    sine = jnp.concatenate([-sine, sine, rest], axis=1)
-
     vmem = pl.BlockSpec(memory_space=pltpu.VMEM)
-    hbm = pl.BlockSpec(memory_space=pl.ANY)
+    free = pl.BlockSpec(memory_space=pl.ANY)
+    hbm = pl.BlockSpec(memory_space=pltpu.HBM)
     dma = pltpu.SemaphoreType.DMA
     return pl.pallas_call(
         kernel,
@@ -286,7 +326,7 @@
             jax.ShapeDtypeStruct((quarter, QL), jnp.bfloat16),
             jax.ShapeDtypeStruct((quarter, KVL + ROPE), jnp.bfloat16),
         ),
-        in_specs=[hbm, hbm, vmem, vmem, vmem, vmem, vmem],
+        in_specs=[hbm, free, hbm, hbm, hbm],
         out_specs=(vmem, vmem),
         scratch_shapes=[
             pltpu.VMEM((4, ROWS, KS), jnp.bfloat16),
@@ -296,16 +336,22 @@
             pltpu.VMEM((ROWS, 128), jnp.float32),
             pltpu.VMEM((4, QUARTER, WIDE), jnp.bfloat16),
             pltpu.VMEM((4, QUARTER, WIDE), jnp.bfloat16),
-            dma((2,)),
+            pltpu.VMEM((D,), jnp.float32),
+            pltpu.VMEM((QL,), jnp.float32),
+            pltpu.VMEM((KVL,), jnp.float32),
+            pltpu.VMEM((QUARTER, 128), jnp.float32),
+            pltpu.VMEM((QUARTER, 128), jnp.float32),
+            dma((5,)),
             dma((6,)), dma((6,)),
             dma((HOPS * PARTS,)), dma((HOPS * PARTS,)),
             dma((HOPS * PARTS,)), dma((HOPS * PARTS,)),
-            dma(((2 * HOPS - 1) * PARTS,)), dma(((2 * HOPS - 1) * PARTS,)),
+            dma((2 * HOPS - 1,)), dma((2 * HOPS - 1,)),
             dma((4,)), dma((4,)),
+            pltpu.SemaphoreType.REGULAR((4,)),
         ],
-        compiler_params=pltpu.CompilerParams(collective_id=0, has_side_effects=True, vmem_limit_bytes=50 * 2**20),
+        compiler_params=pltpu.CompilerParams(collective_id=0, has_side_effects=True, vmem_limit_bytes=56_000_000),
     )(
-        hidden, down_weight, attn_gain.reshape(4, 1, KS), q_gain.reshape(1, QL), kv_gain.reshape(1, KVL), cosine, sine,
+        hidden, down_weight, attn_gain, q_gain, kv_gain,
     )
 
 

time: 72.7 us -> 64.5 us (0.89)
  Pallas kernels: 67 us -> 59.7 us
  local copies, waits for them, and re-layouts: 4.02 us -> 3.17 us
    pallas_call x1, Pallas kernels: 67 us -> 59.7 us  [on_device(): pl.pallas_call(kernel, out_shape=(jax.ShapeDtypeStruct((quarter, QL), jnp...]
    unnamed x11 -> x9, local copies, waits for them, and re-layouts: 3.23 us -> 3.17 us
where the time goes in v2:
time: 64.5 us; the launch traced here: 63.5 us
  Pallas kernels  59.7 us (93%)
  local copies, waits for them, and re-layouts  3.17 us (5%)
  between operations  0.67 us (1%)
    pallas_call x1, Pallas kernels, on_device(): pl.pallas_call(kernel, out_shape=(jax.ShapeDtypeStruct((quarter, QL), jnp...  59.7 us
    unnamed x9, local copies, waits for them, and re-layouts  3.17 us

profile of v2, /device:TPU:6, one launch (start us, length us, event | category | flops | bytes accessed | tf_op | source)
XLA Modules:
  0.0 63.5 jit_solution(744872576889051989)
XLA Ops:
  0.6 0.0 copy-start.2
  0.6 0.0 copy-start.1
  0.7 0.0 copy-start
  0.7 1.8 %copy.7.w = bf16[224,528]{1,0:T(8,128)(2,1)} copy(bf16[224,528]{0,1:T(8,128)(2,1)} %param.9) | data formatting | bytes 473088 | tf_op args[4]
  2.5 0.0 copy-done.2
  2.5 0.0 copy-done.1
  2.5 0.0 copy-done
  2.5 59.7 %shard_map.68 = (bf16[64,1536]{1,0:T(8,128)(2,1)S(1)}, bf16[64,576]{1,0:T(8,128)(2,1)S(1)}) custom-call(bf16[256,1792]{1,0:T(8,128)(2,1)} %hid.1, bf16[224,528]{1,0:T(8,128)(2,1)} %copy.7.w, f32[7168]{0:T(1024)S(1)} %copy-done, f32[1536]{0:T(1024)S(1)} %copy-done.1, f32[512]{0:T(512)S(1)} %copy-done.2), custom_call_target="tpu_custom_call" | custom-call | tf_op jit(solution)/shard_map/pallas_call | solution.py:323
  62.2 0.7 %copy.10 = bf16[64,1536]{1,0:T(8,128)(2,1)} copy(bf16[64,1536]{1,0:T(8,128)(2,1)S(1)} %get-tuple-element.4) | data formatting | bytes 393216
  62.9 0.6 copy.11
Async XLA Ops:
  0.6 1.9 %copy-start.2 = (f32[512]{0:T(512)S(1)}, f32[512]{0:T(512)}, u32[]{:S(2)}) copy-start(f32[512]{0:T(512)} %kv_gain.1) | copy-start | bytes 6148
  0.6 1.9 %copy-start.1 = (f32[1536]{0:T(1024)S(1)}, f32[1536]{0:T(1024)}, u32[]{:S(2)}) copy-start(f32[1536]{0:T(1024)} %q_gain.1) | copy-start | bytes 18436
  0.7 1.9 %copy-start = (f32[7168]{0:T(1024)S(1)}, f32[7168]{0:T(1024)}, u32[]{:S(2)}) copy-start(f32[7168]{0:T(1024)} %gain.1) | copy-start | bytes 86020

commit v3 on v2

--- a/solution.py
+++ b/solution.py
@@ -24,6 +24,7 @@
 WC = 528
 PARTS = 7
 PR = WR // PARTS
+GROUP = 4 * WR
 HALF = ROWS // 2
 QUARTER = ROWS // 4
 WIDE = 640
@@ -102,14 +103,8 @@
     def ring_slot(d):
         return yl * NZ + (z - way * d + NZ) % NZ
 
-    def pair_slot(j):
-        return (1 - yl) * NZ + (z - way * (j + 1 - core) + NZ) % NZ
-
-    def cross_ring_slot(d):
-        return yl * NZ + (z + way * d + NZ) % NZ
-
-    def cross_pair_slot(j):
-        return (1 - yl) * NZ + (z + way * (j + core) + NZ) % NZ
+    def pair_slot(d):
+        return (1 - yl) * NZ + (z - way * d + NZ) % NZ
 
     def w_src(d, part):
         if d == 0:
@@ -129,13 +124,8 @@
         return rdma(w_src(d, part), w_rows(ring_slot(d), part), zs.at[i], zr.at[i], ahead_z)
 
     def y_copy(d, part):
-        i = (d - 1 + core) * PARTS + part
+        i = d * PARTS + part
         return rdma(w_src(d, part), w_rows(ring_slot(d), part), ys.at[i], yr.at[i], ahead_y)
-
-    def diagonal(part):
-        i = (HOPS - 1) * PARTS + part
-        rows = w_rows(ring_slot(HOPS - 1), part)
-        return rdma(rows, rows, ys.at[i], yr.at[i], place(y + way, z + way, core, x))
 
     def shard(slot):
         return wbuf.at[pl.ds(pl.multiple_of(slot * WR, WR), WR)]
@@ -150,14 +140,17 @@
 
         lax.fori_loop(0, PARTS, body, 0)
 
-    def hand_on_pair(j):
+    def await_pair(d):
         def step(part):
-            i = j * PARTS + part
-            rows = w_rows(pair_slot(j), part)
+            i = d * PARTS + part
+            rows = w_rows(0, 0)
             rdma(rows, rows, ys.at[i], yr.at[i], ahead_y).wait_recv()
 
         each_part(step)
-        start(cross(pair_slot(j), HOPS - 1 + j))
+
+    def hand_on_pair(d):
+        await_pair(d)
+        cross(pair_slot(d), HOPS - 1 + d).start()
 
     def angles():
         half_rope = ROPE // 2
@@ -185,11 +178,25 @@
 
         lax.fori_loop(0, HALF // 16, block, 0)
 
-    def multiply(owner):
-        columns = wbuf[pl.ds(pl.multiple_of(owner * KS, KS), KS), :]
+    def multiply(parity, z_from):
+        group = parity * (NZ // 4) + z_from % NZ // 4
+        owner = group // 2
+        depth = pl.ds(pl.multiple_of(group % 2 * GROUP, GROUP), GROUP)
+        columns = wbuf[pl.ds(pl.multiple_of(group * GROUP, GROUP), GROUP), :]
         for half in range(2):
             rows = pl.ds(half * HALF, HALF)
-            acc[rows, :WC] += jnp.dot(xg[owner, rows, :], columns, preferred_element_type=jnp.float32)
+            acc[rows, :WC] += jnp.dot(xg[owner, rows, depth], columns, preferred_element_type=jnp.float32)
+
+    def multiply_all(parity, first_step, last_step):
+        def body(i, carry):
+            multiply(parity, z + 4 * i)
+            return carry
+
+        lax.fori_loop(first_step, last_step + 1, body, 0)
+
+    def await_cross(first_index, last_index):
+        for i in range(first_index, last_index + 1):
+            cross(0, i).wait_recv()
 
     def first(part):
         z_copy(0, part).start()
@@ -223,19 +230,19 @@
             z_copy(d - 1, part).wait_recv()
             if d < HOPS:
                 z_copy(d, part).start()
-                if d == HOPS - 1:
-
-                    @pl.when(core == 0)
-                    def _():
-                        diagonal(part).start()
-
-                y_copy(d, part).start()
+            y_copy(d, part).start()
 
         each_part(step)
         if d < HOPS:
             start(cross(ring_slot(d), d - 1))
+        if d == 2:
+
+            @pl.when(core == 1)
+            def _():
+                hand_on_pair(0)
+
         if d >= 3:
-            hand_on_pair(d - 3)
+            hand_on_pair(d - 2)
         if d <= 4:
             next_round(d - 1)
         if d == 5:
@@ -245,30 +252,28 @@
             start(rdma(x_rows(x_right, 1), x_rows(x_right, 1), xs.at[5], xr.at[5], left))
         if d == 6:
             prepare(x_left, 0)
+            prepare(x_right, 1)
         if d == 7:
-            prepare(x_right, 1)
-    hand_on_pair(HOPS - 2)
+            x_own(1, 2, right).wait_recv()
+            prepare(x_left, 1)
+            x_own(0, 3, left).wait_recv()
+            prepare(x_right, 0)
     hand_on_pair(HOPS - 1)
-
-    x_own(1, 2, right).wait_recv()
-    prepare(x_left, 1)
-    x_own(0, 3, left).wait_recv()
-    prepare(x_right, 0)
-
-    for i in range(2 * HOPS - 1):
-        cross(0, i).wait_recv()
-
-    def slice_step(i, carry):
-        multiply(lax.rem(x_left + i, 4))
-        return carry
-
-    lax.fori_loop(0, 3, slice_step, 0)
-
     for half in range(2):
         rows = x_rows(x_far, half)
         rdma(rows, rows, xs.at[4 + half], xr.at[4 + half], right).wait_recv()
         prepare(x_far, half)
-    multiply(x_far)
+    await_cross(0, HOPS - 2)
+    multiply_all(yl, 0, 3)
+
+    @pl.when(core == 0)
+    def _():
+        await_cross(HOPS - 1, HOPS - 1)
+
+    await_cross(HOPS, 2 * HOPS - 2)
+    multiply_all(1 - yl, 3, 5)
+    await_pair(HOPS)
+    multiply_all(1 - yl, 6, 6)
 
     scale = lax.rsqrt(jnp.sum(ssq[...], axis=1, keepdims=True) / D + epsilon)
     out = pltpu.roll(acc[...] * scale, x * 16, 1).astype(jnp.bfloat16)
@@ -308,10 +313,19 @@
     def sent(i, carry):
         rows = w_rows(0, 0)
         rdma(rows, rows, zs.at[i], zr.at[i], ahead_z).wait_send()
-        rdma(rows, rows, ys.at[i], yr.at[i], ahead_y).wait_send()
+        rdma(rows, rows, ys.at[PARTS + i], yr.at[PARTS + i], ahead_y).wait_send()
         return carry
 
     lax.fori_loop(0, HOPS * PARTS, sent, 0)
+    for d in range(1, HOPS):
+        cross(0, HOPS - 1 + d).wait_send()
+
+    @pl.when(core == 1)
+    def _():
+        for part in range(PARTS):
+            rows = w_rows(0, 0)
+            rdma(rows, rows, ys.at[part], yr.at[part], ahead_y).wait_send()
+        cross(0, HOPS - 1).wait_send()
 
 
 def on_device(hidden, attn_gain, q_gain, kv_gain, down_weight):
@@ -344,7 +358,7 @@
             dma((5,)),
             dma((6,)), dma((6,)),
             dma((HOPS * PARTS,)), dma((HOPS * PARTS,)),
-            dma((HOPS * PARTS,)), dma((HOPS * PARTS,)),
+            dma(((HOPS + 1) * PARTS,)), dma(((HOPS + 1) * PARTS,)),
             dma((2 * HOPS - 1,)), dma((2 * HOPS - 1,)),
             dma((4,)), dma((4,)),
             pltpu.SemaphoreType.REGULAR((4,)),

time: 64.5 us -> 61.3 us (0.950)
  Pallas kernels: 59.7 us -> 57 us
    pallas_call x1, Pallas kernels: 59.7 us -> 57 us  [on_device(): pl.pallas_call(kernel, out_shape=(jax.ShapeDtypeStruct((quarter, QL), jnp...]
where the time goes in v3:
time: 61.3 us; the launch traced here: 60.9 us
  Pallas kernels  57 us (93%)
  local copies, waits for them, and re-layouts  3.17 us (5%)
  between operations  0.67 us (1%)
    pallas_call x1, Pallas kernels, on_device(): pl.pallas_call(kernel, out_shape=(jax.ShapeDtypeStruct((quarter, QL), jnp...  57 us
    unnamed x9, local copies, waits for them, and re-layouts  3.17 us

profile of v3, /device:TPU:6, one launch (start us, length us, event | category | flops | bytes accessed | tf_op | source)
XLA Modules:
  0.0 60.9 jit_solution(3437623712005208287)
XLA Ops:
  0.6 0.0 copy-start.2
  0.6 0.0 copy-start.1
  0.7 0.0 copy-start
  0.7 1.8 %copy.7.w = bf16[224,528]{1,0:T(8,128)(2,1)} copy(bf16[224,528]{0,1:T(8,128)(2,1)} %param.9) | data formatting | bytes 473088 | tf_op args[4]
  2.5 0.0 copy-done.2
  2.5 0.0 copy-done.1
  2.5 0.0 copy-done
  2.5 57.0 %shard_map.68 = (bf16[64,1536]{1,0:T(8,128)(2,1)S(1)}, bf16[64,576]{1,0:T(8,128)(2,1)S(1)}) custom-call(bf16[256,1792]{1,0:T(8,128)(2,1)} %hid.1, bf16[224,528]{1,0:T(8,128)(2,1)} %copy.7.w, f32[7168]{0:T(1024)S(1)} %copy-done, f32[1536]{0:T(1024)S(1)} %copy-done.1, f32[512]{0:T(512)S(1)} %copy-done.2), custom_call_target="tpu_custom_call" | custom-call | tf_op jit(solution)/shard_map/pallas_call | solution.py:337
  59.5 0.7 %copy.10 = bf16[64,1536]{1,0:T(8,128)(2,1)} copy(bf16[64,1536]{1,0:T(8,128)(2,1)S(1)} %get-tuple-element.4) | data formatting | bytes 393216
  60.2 0.6 %copy.11 = bf16[64,576]{1,0:T(8,128)(2,1)} copy(bf16[64,576]{1,0:T(8,128)(2,1)S(1)} %get-tuple-element.5) | data formatting | bytes 147456
Async XLA Ops:
  0.6 1.9 %copy-start.2 = (f32[512]{0:T(512)S(1)}, f32[512]{0:T(512)}, u32[]{:S(2)}) copy-start(f32[512]{0:T(512)} %kv_gain.1) | copy-start | bytes 6148
  0.6 1.9 %copy-start.1 = (f32[1536]{0:T(1024)S(1)}, f32[1536]{0:T(1024)}, u32[]{:S(2)}) copy-start(f32[1536]{0:T(1024)} %q_gain.1) | copy-start | bytes 18436
  0.7 1.9 %copy-start = (f32[7168]{0:T(1024)S(1)}, f32[7168]{0:T(1024)}, u32[]{:S(2)}) copy-start(f32[7168]{0:T(1024)} %gain.1) | copy-start | bytes 86020

commit v4 on v3

--- a/solution.py
+++ b/solution.py
@@ -183,9 +183,10 @@
         owner = group // 2
         depth = pl.ds(pl.multiple_of(group % 2 * GROUP, GROUP), GROUP)
         columns = wbuf[pl.ds(pl.multiple_of(group * GROUP, GROUP), GROUP), :]
-        for half in range(2):
-            rows = pl.ds(half * HALF, HALF)
-            acc[rows, :WC] += jnp.dot(xg[owner, rows, depth], columns, preferred_element_type=jnp.float32)
+        acc[:, :WC] += jnp.dot(xg[owner, :, depth], columns, preferred_element_type=jnp.float32)
+
+    def near_owner(parity):
+        return (parity * (NZ // 4) + z // 4) // 2
 
     def multiply_all(parity, first_step, last_step):
         def body(i, carry):
@@ -258,20 +259,41 @@
             prepare(x_left, 1)
             x_own(0, 3, left).wait_recv()
             prepare(x_right, 0)
+            await_cross(0, 2)
+
+            @pl.when(near_owner(yl) != x_far)
+            def _():
+                multiply(yl, z)
+
+            @pl.when(core == 0)
+            def _():
+                await_cross(HOPS - 1, HOPS - 1)
+
+            await_cross(HOPS, HOPS + 2)
+
+            @pl.when(near_owner(1 - yl) != x_far)
+            def _():
+                multiply(1 - yl, z)
+
     hand_on_pair(HOPS - 1)
     for half in range(2):
         rows = x_rows(x_far, half)
         rdma(rows, rows, xs.at[4 + half], xr.at[4 + half], right).wait_recv()
         prepare(x_far, half)
-    await_cross(0, HOPS - 2)
-    multiply_all(yl, 0, 3)
-
-    @pl.when(core == 0)
+    @pl.when(near_owner(yl) == x_far)
     def _():
-        await_cross(HOPS - 1, HOPS - 1)
-
-    await_cross(HOPS, 2 * HOPS - 2)
-    multiply_all(1 - yl, 3, 5)
+        multiply(yl, z)
+
+    @pl.when(near_owner(1 - yl) == x_far)
+    def _():
+        multiply(1 - yl, z)
+
+    await_cross(3, HOPS - 2)
+    multiply_all(yl, 1, 3)
+
+    await_cross(HOPS + 3, 2 * HOPS - 2)
+    multiply_all(1 - yl, 3, 3)
+    multiply_all(1 - yl, 5, 5)
     await_pair(HOPS)
     multiply_all(1 - yl, 6, 6)
 

time: 61.3 us -> 60 us (0.979)
  Pallas kernels: 57 us -> 56 us
    pallas_call x1, Pallas kernels: 57 us -> 56 us  [on_device(): pl.pallas_call(kernel, out_shape=(jax.ShapeDtypeStruct((quarter, QL), jnp...]
where the time goes in v4:
time: 60 us; the launch traced here: 59.8 us
  Pallas kernels  56 us (93%)
  local copies, waits for them, and re-layouts  3.17 us (5%)
  between operations  0.67 us (1%)
    pallas_call x1, Pallas kernels, on_device(): pl.pallas_call(kernel, out_shape=(jax.ShapeDtypeStruct((quarter, QL), jnp...  56 us
    unnamed x9, local copies, waits for them, and re-layouts  3.17 us

profile of v4, /device:TPU:6, one launch (start us, length us, event | category | flops | bytes accessed | tf_op | source)
XLA Modules:
  0.0 59.8 jit_solution(515102615370603403)
XLA Ops:
  0.6 0.0 copy-start.2
  0.6 0.0 copy-start.1
  0.7 0.0 copy-start
  0.7 1.8 %copy.7.w = bf16[224,528]{1,0:T(8,128)(2,1)} copy(bf16[224,528]{0,1:T(8,128)(2,1)} %param.9) | data formatting | bytes 473088 | tf_op args[4]
  2.5 0.0 copy-done.2
  2.5 0.0 copy-done.1
  2.5 0.0 copy-done
  2.5 56.0 %shard_map.68 = (bf16[64,1536]{1,0:T(8,128)(2,1)S(1)}, bf16[64,576]{1,0:T(8,128)(2,1)S(1)}) custom-call(bf16[256,1792]{1,0:T(8,128)(2,1)} %hid.1, bf16[224,528]{1,0:T(8,128)(2,1)} %copy.7.w, f32[7168]{0:T(1024)S(1)} %copy-done, f32[1536]{0:T(1024)S(1)} %copy-done.1, f32[512]{0:T(512)S(1)} %copy-done.2), custom_call_target="tpu_custom_call" | custom-call | tf_op jit(solution)/shard_map/pallas_call | solution.py:359
  58.5 0.7 %copy.10 = bf16[64,1536]{1,0:T(8,128)(2,1)} copy(bf16[64,1536]{1,0:T(8,128)(2,1)S(1)} %get-tuple-element.4) | data formatting | bytes 393216
  59.2 0.6 %copy.11 = bf16[64,576]{1,0:T(8,128)(2,1)} copy(bf16[64,576]{1,0:T(8,128)(2,1)S(1)} %get-tuple-element.5) | data formatting | bytes 147456
Async XLA Ops:
  0.6 1.9 %copy-start.2 = (f32[512]{0:T(512)S(1)}, f32[512]{0:T(512)}, u32[]{:S(2)}) copy-start(f32[512]{0:T(512)} %kv_gain.1) | copy-start | bytes 6148
  0.6 1.9 %copy-start.1 = (f32[1536]{0:T(1024)S(1)}, f32[1536]{0:T(1024)}, u32[]{:S(2)}) copy-start(f32[1536]{0:T(1024)} %q_gain.1) | copy-start | bytes 18436
  0.7 1.9 %copy-start = (f32[7168]{0:T(1024)S(1)}, f32[7168]{0:T(1024)}, u32[]{:S(2)}) copy-start(f32[7168]{0:T(1024)} %gain.1) | copy-start | bytes 86020
